TPU v7x, 256 devices: a whole 4x4x8 slice. The times are simulated.
256 devices in a mesh: rep: 8 (over y, x_hi), blk: 32 (over z, x_lo, core).
Axes of the slice: x: 4 (x_hi: 2, x_lo: 2; x = x_hi * 2 + x_lo), y: 4, z: 8, core: 2. Of those that a mesh axis runs over, the one named last changes fastest.
Arguments:
- features: bfloat16 [131072, 128], P(('rep', 'blk')), may hold values from -6 to 6
- degrees: int32 [131072], P(('rep', 'blk')), may hold values from 1 to 32
- tile_weights: bfloat16 [8, 32, 320, 128, 128], P('rep', 'blk'), may hold values from 0 to 0.049804688
- tile_rows: int32 [8, 32, 320], P('rep', 'blk'), may hold values from 0 to 127, as said below
- tile_cols: int32 [8, 32, 320], P('rep', 'blk'), may hold values from 0 to 31, as said below
- tile_counts: int32 [8, 32], P('rep', 'blk'), may hold values from 1 to 320, as said below
- weight: bfloat16 [128, 256], replicated, may hold values from -0.5 to 0.5
- layer_bias: float32 [256], replicated, may hold values from -3 to 3
- upstream: bfloat16 [131072, 256], P(('rep', 'blk')), may hold values from -6 to 6
Outputs:
- hidden: bfloat16 [131072, 256], P(('rep', 'blk'))
- feature_grad: bfloat16 [131072, 128], P(('rep', 'blk'))
- weight_grad: float32 [128, 256], replicated
- bias_grad: float32 [256], replicated
Inputs may be any that keep to these rules, and one draw needn't show every extreme that they name: `tile_rows`: the first tile_counts slots of a device hold distinct tiles, ordered by row and then by column; a used row h lies in node block r * 32 + h // 4, whose index h // 4 is within 3 steps of the device's blk index around the loop of 32; unused slots hold the device's own first tile row. `tile_cols`: unused slots hold 0. `tile_counts`: at most 80 used slots of one device lie in the rows of one node block; this and the largest count are both reached by some device in every draw.
All inputs are finite; a program needn't handle non-finite values.
Results may differ from a plain program's by a relative error of at most 0.015.
Values may be sent and summed in bfloat16 or wider, within the bound.
A program may use at most 128 MiB of HBM per device.

v0:
```python
import jax
import jax.numpy as jnp
from jax import lax
from jax.sharding import PartitionSpec as P

REACH = 3


def shifted(value, axis, by):
    length = lax.axis_size(axis)
    return lax.ppermute(value, axis, [(i, (i + by) % length) for i in range(length)])


def node_scale(degrees):
    return 1.0 / jnp.sqrt(degrees.astype(jnp.float32) + 1.0)


def on_device(
    features, degrees, tile_weights, tile_rows, tile_cols, tile_counts, weight, layer_bias, upstream
):
    row_count, feat_width = features.shape
    tile_size = tile_weights.shape[-1]
    slot_total = tile_weights.shape[2]
    row_tiles = row_count // tile_size
    rep_count = lax.axis_size("rep")
    blk_count = lax.axis_size("blk")
    blk_index = lax.axis_index("blk")
    window_blocks = 2 * REACH + 1
    window_tiles = window_blocks * row_tiles
    column_tiles = rep_count * row_tiles
    slot_block = slot_total // (2 * (REACH + 1))
    block_total = slot_total // slot_block
    weights_dev = tile_weights[0, 0]
    rows_dev = tile_rows[0, 0]
    cols_dev = tile_cols[0, 0]
    count_dev = tile_counts[0, 0]
    group_index = rows_dev // row_tiles
    distance = (group_index - blk_index) % blk_count
    distance = jnp.where(distance > blk_count // 2, distance - blk_count, distance)
    window_rows = (distance + REACH) * row_tiles + rows_dev % row_tiles
    slot_ids = jnp.arange(slot_total, dtype=jnp.int32)
    slot_valid = slot_ids < count_dev
    window_seg = jnp.where(slot_valid, window_rows, window_tiles)
    column_seg = jnp.where(slot_valid, cols_dev, column_tiles)

    def tile_pass(source_tiles, gather_index, segment_index, segment_total, pattern):

        def add_block(block_id, running):
            slot_first = block_id * slot_block
            weights_part = lax.dynamic_slice_in_dim(weights_dev, slot_first, slot_block, 0)
            gather_part = lax.dynamic_slice_in_dim(gather_index, slot_first, slot_block, 0)
            segment_part = lax.dynamic_slice_in_dim(segment_index, slot_first, slot_block, 0)
            products = jnp.einsum(
                pattern, weights_part, source_tiles[gather_part], preferred_element_type=jnp.float32
            )
            return (
                running
                + jax.ops.segment_sum(products, segment_part, segment_total + 1)[:segment_total]
            )

        zero_sum = jnp.zeros((segment_total, tile_size, feat_width), jnp.float32)
        return lax.fori_loop(0, block_total, add_block, zero_sum)

    node_norm = node_scale(degrees)
    scaled = (node_norm[:, None] * features.astype(jnp.float32)).astype(jnp.bfloat16)
    source_rows = lax.all_gather(scaled, "rep", axis=0, tiled=True)
    source_tiles = source_rows.reshape(column_tiles, tile_size, feat_width)
    partial_value = tile_pass(source_tiles, cols_dev, window_seg, window_tiles, "tab,tbf->taf")
    partial_value = partial_value.reshape(window_blocks, row_count, feat_width)
    neighbor_sum = partial_value[REACH]
    for offset in range(-REACH, REACH + 1):
        if offset != 0:
            neighbor_sum = neighbor_sum + shifted(
                partial_value[offset + REACH].astype(jnp.bfloat16), "blk", offset
            ).astype(jnp.float32)
    aggregated = (node_norm[:, None] * (neighbor_sum + scaled.astype(jnp.float32))).astype(
        jnp.bfloat16
    )
    pre_act = jnp.dot(aggregated, weight, preferred_element_type=jnp.float32) + layer_bias
    hidden = jax.nn.silu(pre_act).astype(jnp.bfloat16)
    gate_sigmoid = jax.nn.sigmoid(pre_act)
    pre_grad = (
        upstream.astype(jnp.float32)
        * (gate_sigmoid + pre_act * gate_sigmoid * (1.0 - gate_sigmoid))
    ).astype(jnp.bfloat16)
    local_weight = jnp.dot(aggregated.T, pre_grad, preferred_element_type=jnp.float32)
    local_bias = jnp.sum(pre_grad.astype(jnp.float32), axis=0)
    weight_sum, bias_sum = lax.psum((local_weight, local_bias), ("rep", "blk"))
    grad_scale = (row_count * rep_count * blk_count) ** (-0.5)
    scaled_grad = (
        node_norm[:, None] * jnp.dot(pre_grad, weight.T, preferred_element_type=jnp.float32)
    ).astype(jnp.bfloat16)
    window_parts = [scaled_grad] * window_blocks
    for offset in range(-REACH, REACH + 1):
        if offset != 0:
            window_parts[offset + REACH] = shifted(scaled_grad, "blk", -offset)
    grad_tiles = jnp.stack(window_parts).reshape(window_tiles, tile_size, feat_width)
    column_part = tile_pass(grad_tiles, window_rows, column_seg, column_tiles, "tab,taf->tbf")
    column_sum = lax.psum_scatter(
        column_part.reshape(rep_count * row_count, feat_width).astype(jnp.bfloat16),
        "rep",
        scatter_dimension=0,
        tiled=True,
    ).astype(jnp.float32)
    feature_grad = (node_norm[:, None] * (column_sum + scaled_grad.astype(jnp.float32))).astype(
        jnp.bfloat16
    )
    return (hidden, feature_grad, weight_sum * grad_scale, bias_sum * grad_scale)


def solution(mesh):
    placed = (
        P(("rep", "blk"), None),
        P(("rep", "blk")),
        P("rep", "blk", None, None, None),
        P("rep", "blk", None),
        P("rep", "blk", None),
        P("rep", "blk"),
        P(),
        P(),
        P(("rep", "blk"), None),
    )
    return jax.shard_map(
        on_device,
        mesh=mesh,
        in_specs=placed,
        out_specs=(P(("rep", "blk"), None), P(("rep", "blk"), None), P(), P()),
        check_vma=False,
    )
```

profile of v0, /device:TPU:32, one launch (start us, length us, event | category | flops | bytes accessed | tf_op | source)
XLA Modules:
  0.0 557.3 jit_solution(4385618830677992955)
XLA Ops:
  11.8 53.4 %all-gather.2.cloned.1.call-done = bf16[4096,128]{1,0:T(8,128)(2,1)} async-done(((bf16[512,128]{1,0:T(8,128)(2,1)}), bf16[4096,128]{1,0:T(8,128)(2,1)}) %all-gather.2.cloned.1.call-update) | async-done | bytes 1048592 | tf_op jit(solution)/shard_map/all_gather | solution.py:66
  65.2 120.4 %while.28 = (s32[]{:T(128)}, f32[28,128,128]{2,1,0:T(8,128)}, s32[320]{0:T(512)S(1)}, bf16[320,128,128]{2,1,0:T(8,128)(2,1)}, s32[320]{0:T(512)S(1)}, /*index=5*...) while((s32[]{:T(128)}, f32[28,128,128]{2,1,0:T(8,128)}, ...), condition=%wide.region_2.3_spmd.clone, body=%wide.region_0.2_spmd.clone.sunk | while | flops 169346176 | bytes 23139612 | solution.py:62
  67.4 3.3 fusion.44
  71.0 6.5 %scatter_fusion = f32[29,128,128]{2,1,0:T(8,128)S(1)} fusion(f32[29,128,128]{2,1,0:T(8,128)S(1)} %broadcast.127, s32[40]{0:T(128)S(1)} %dynamic_slice.62, f32[40,128,128]{2,1,0:T(8,128)} %fusion.44), kind=kCustom, calls=%fused_computation.2.clone.clone.1 | custom fusion | flops 655360 | bytes 7864480 | tf_op jit(solution)/shard_map/while/body/eval_jaxpr/scatter-add | solution.py:58
  81.2 3.3 fusion.44
  84.7 6.5 %scatter_fusion = f32[29,128,128]{2,1,0:T(8,128)S(1)} fusion(f32[29,128,128]{2,1,0:T(8,128)S(1)} %broadcast.127, s32[40]{0:T(128)S(1)} %dynamic_slice.62, f32[40,128,128]{2,1,0:T(8,128)} %fusion.44), kind=kCustom, calls=%fused_computation.2.clone.clone.1 | custom fusion | flops 655360 | bytes 7864480 | tf_op jit(solution)/shard_map/while/body/eval_jaxpr/scatter-add | solution.py:58
  100.0 6.5 %scatter_fusion = f32[29,128,128]{2,1,0:T(8,128)S(1)} fusion(f32[29,128,128]{2,1,0:T(8,128)S(1)} %broadcast.127, s32[40]{0:T(128)S(1)} %dynamic_slice.62, f32[40,128,128]{2,1,0:T(8,128)} %fusion.44), kind=kCustom, calls=%fused_computation.2.clone.clone.1 | custom fusion | flops 655360 | bytes 7864480 | tf_op jit(solution)/shard_map/while/body/eval_jaxpr/scatter-add | solution.py:58
  115.2 6.5 %scatter_fusion = f32[29,128,128]{2,1,0:T(8,128)S(1)} fusion(f32[29,128,128]{2,1,0:T(8,128)S(1)} %broadcast.127, s32[40]{0:T(128)S(1)} %dynamic_slice.62, f32[40,128,128]{2,1,0:T(8,128)} %fusion.44), kind=kCustom, calls=%fused_computation.2.clone.clone.1 | custom fusion | flops 655360 | bytes 7864480 | tf_op jit(solution)/shard_map/while/body/eval_jaxpr/scatter-add | solution.py:58
  130.4 6.5 %scatter_fusion = f32[29,128,128]{2,1,0:T(8,128)S(1)} fusion(f32[29,128,128]{2,1,0:T(8,128)S(1)} %broadcast.127, s32[40]{0:T(128)S(1)} %dynamic_slice.62, f32[40,128,128]{2,1,0:T(8,128)} %fusion.44), kind=kCustom, calls=%fused_computation.2.clone.clone.1 | custom fusion | flops 655360 | bytes 7864480 | tf_op jit(solution)/shard_map/while/body/eval_jaxpr/scatter-add | solution.py:58
  145.7 6.5 %scatter_fusion = f32[29,128,128]{2,1,0:T(8,128)S(1)} fusion(f32[29,128,128]{2,1,0:T(8,128)S(1)} %broadcast.127, s32[40]{0:T(128)S(1)} %dynamic_slice.62, f32[40,128,128]{2,1,0:T(8,128)} %fusion.44), kind=kCustom, calls=%fused_computation.2.clone.clone.1 | custom fusion | flops 655360 | bytes 7864480 | tf_op jit(solution)/shard_map/while/body/eval_jaxpr/scatter-add | solution.py:58
  157.4 3.3 fusion.44
  160.9 6.5 %scatter_fusion = f32[29,128,128]{2,1,0:T(8,128)S(1)} fusion(f32[29,128,128]{2,1,0:T(8,128)S(1)} %broadcast.127, s32[40]{0:T(128)S(1)} %dynamic_slice.62, f32[40,128,128]{2,1,0:T(8,128)} %fusion.44), kind=kCustom, calls=%fused_computation.2.clone.clone.1 | custom fusion | flops 655360 | bytes 7864480 | tf_op jit(solution)/shard_map/while/body/eval_jaxpr/scatter-add | solution.py:58
  172.6 3.3 fusion.44
  176.2 6.5 %scatter_fusion = f32[29,128,128]{2,1,0:T(8,128)S(1)} fusion(f32[29,128,128]{2,1,0:T(8,128)S(1)} %broadcast.127, s32[40]{0:T(128)S(1)} %dynamic_slice.62, f32[40,128,128]{2,1,0:T(8,128)} %fusion.44), kind=kCustom, calls=%fused_computation.2.clone.clone.1 | custom fusion | flops 655360 | bytes 7864480 | tf_op jit(solution)/shard_map/while/body/eval_jaxpr/scatter-add | solution.py:58
  187.5 14.4 %copy.13 = bf16[1,1,320,128,128]{3,4,2,1,0:T(8,128)(2,1)} copy(bf16[1,1,320,128,128]{4,3,2,1,0:T(8,128)(2,1)} %bitcast.61) | data formatting | bytes 20971520 | tf_op args[2]
  209.3 4.0 collective-permute-done.4
  223.9 5.1 collective-permute-done.6
  230.9 5.0 collective-permute-done.7
  236.2 113.0 %while.29 = (s32[]{:T(128)}, f32[32,128,128]{2,1,0:T(8,128)}, s32[320]{0:T(512)S(1)}, bf16[320,128,128]{1,2,0:T(8,128)(2,1)}, s32[320]{0:T(512)S(1)}, /*index=5*...) while((s32[]{:T(128)}, f32[32,128,128]{2,1,0:T(8,128)}, ...), condition=%wide.region_5.6_spmd.clone, body=%wide.region_3.5_spmd.clone.sunk | while | flops 169477248 | bytes 24188188 | solution.py:62
  240.7 6.6 %scatter_fusion.1 = f32[33,128,128]{2,1,0:T(8,128)S(1)} fusion(f32[33,128,128]{2,1,0:T(8,128)S(1)} %broadcast.134, s32[40]{0:T(128)S(1)} %dynamic_slice.65, f32[40,128,128]{2,1,0:T(8,128)} %fusion.47), kind=kCustom, calls=%fused_computation.3.clone.clone.1 | custom fusion | flops 655360 | bytes 7864480 | tf_op jit(solution)/shard_map/while/body/eval_jaxpr/scatter-add | solution.py:58
  253.5 6.6 %scatter_fusion.1 = f32[33,128,128]{2,1,0:T(8,128)S(1)} fusion(f32[33,128,128]{2,1,0:T(8,128)S(1)} %broadcast.134, s32[40]{0:T(128)S(1)} %dynamic_slice.65, f32[40,128,128]{2,1,0:T(8,128)} %fusion.47), kind=kCustom, calls=%fused_computation.3.clone.clone.1 | custom fusion | flops 655360 | bytes 7864480 | tf_op jit(solution)/shard_map/while/body/eval_jaxpr/scatter-add | solution.py:58
  264.2 3.3 fusion.47
  267.8 6.6 %scatter_fusion.1 = f32[33,128,128]{2,1,0:T(8,128)S(1)} fusion(f32[33,128,128]{2,1,0:T(8,128)S(1)} %broadcast.134, s32[40]{0:T(128)S(1)} %dynamic_slice.65, f32[40,128,128]{2,1,0:T(8,128)} %fusion.47), kind=kCustom, calls=%fused_computation.3.clone.clone.1 | custom fusion | flops 655360 | bytes 7864480 | tf_op jit(solution)/shard_map/while/body/eval_jaxpr/scatter-add | solution.py:58
  278.6 3.3 fusion.47
  282.2 6.6 %scatter_fusion.1 = f32[33,128,128]{2,1,0:T(8,128)S(1)} fusion(f32[33,128,128]{2,1,0:T(8,128)S(1)} %broadcast.134, s32[40]{0:T(128)S(1)} %dynamic_slice.65, f32[40,128,128]{2,1,0:T(8,128)} %fusion.47), kind=kCustom, calls=%fused_computation.3.clone.clone.1 | custom fusion | flops 655360 | bytes 7864480 | tf_op jit(solution)/shard_map/while/body/eval_jaxpr/scatter-add | solution.py:58
  296.5 6.6 %scatter_fusion.1 = f32[33,128,128]{2,1,0:T(8,128)S(1)} fusion(f32[33,128,128]{2,1,0:T(8,128)S(1)} %broadcast.134, s32[40]{0:T(128)S(1)} %dynamic_slice.65, f32[40,128,128]{2,1,0:T(8,128)} %fusion.47), kind=kCustom, calls=%fused_computation.3.clone.clone.1 | custom fusion | flops 655360 | bytes 7864480 | tf_op jit(solution)/shard_map/while/body/eval_jaxpr/scatter-add | solution.py:58
  310.8 6.6 %scatter_fusion.1 = f32[33,128,128]{2,1,0:T(8,128)S(1)} fusion(f32[33,128,128]{2,1,0:T(8,128)S(1)} %broadcast.134, s32[40]{0:T(128)S(1)} %dynamic_slice.65, f32[40,128,128]{2,1,0:T(8,128)} %fusion.47), kind=kCustom, calls=%fused_computation.3.clone.clone.1 | custom fusion | flops 655360 | bytes 7864480 | tf_op jit(solution)/shard_map/while/body/eval_jaxpr/scatter-add | solution.py:58
  325.1 6.5 %scatter_fusion.1 = f32[33,128,128]{2,1,0:T(8,128)S(1)} fusion(f32[33,128,128]{2,1,0:T(8,128)S(1)} %broadcast.134, s32[40]{0:T(128)S(1)} %dynamic_slice.65, f32[40,128,128]{2,1,0:T(8,128)} %fusion.47), kind=kCustom, calls=%fused_computation.3.clone.clone.1 | custom fusion | flops 655360 | bytes 7864480 | tf_op jit(solution)/shard_map/while/body/eval_jaxpr/scatter-add | solution.py:58
  339.4 6.5 %scatter_fusion.1 = f32[33,128,128]{2,1,0:T(8,128)S(1)} fusion(f32[33,128,128]{2,1,0:T(8,128)S(1)} %broadcast.134, s32[40]{0:T(128)S(1)} %dynamic_slice.65, f32[40,128,128]{2,1,0:T(8,128)} %fusion.47), kind=kCustom, calls=%fused_computation.3.clone.clone.1 | custom fusion | flops 655360 | bytes 7864480 | tf_op jit(solution)/shard_map/while/body/eval_jaxpr/scatter-add | solution.py:58
  351.9 75.9 %psum.15 = f32[256]{0:T(256)S(1)} all-reduce(f32[256]{0:T(256)S(1)} %get-tuple-element.296), channel_id=1, replica_groups=mesh['rep'=8,'blk'=32] {'rep','blk'}, use_global_device_ids=true, to_apply=%region_9.10 | all-reduce | flops 256 | bytes 2048 | tf_op jit(solution)/shard_map/psum | solution.py:88
  428.4 41.1 %all-reduce.2.cloned.1.call-done = f32[128,256]{1,0:T(8,128)} async-done(((f32[128,256]{1,0:T(8,128)}), f32[128,256]{1,0:T(8,128)}) %all-reduce.2.cloned.1.call-update) | async-done | bytes 131088 | tf_op jit(solution)/shard_map/psum | solution.py:88
  471.1 77.9 %reduce-scatter.2.cloned.1.call-done = bf16[512,128]{1,0:T(8,128)(2,1)} async-done(((bf16[4096,128]{1,0:T(8,128)(2,1)}), bf16[512,128]{1,0:T(8,128)(2,1)}) %reduce-scatter.2.cloned.1.call-update) | async-done | bytes 131088 | tf_op jit(solution)/shard_map/reduce_scatter | solution.py:99
  (167 shorter events, 140.5 us)
Async XLA Ops:
  7.2 208.5 %copy-start = (bf16[128,256]{1,0:T(8,128)(2,1)S(1)}, bf16[128,256]{1,0:T(8,128)(2,1)}, u32[]{:S(2)}) copy-start(bf16[128,256]{1,0:T(8,128)(2,1)} %param.19) | copy-start | bytes 196612
  7.2 58.0 %all-gather.2.cloned.1.call-start = ((), (), s32[]{:S(2)}) async-start(), calls=%async_computation.1 | async-start | bytes 1179648 | tf_op jit(solution)/shard_map/all_gather | solution.py:66
  9.6 459.9 %all-reduce.2.cloned.1.call-start = ((), (), s32[]{:S(2)}) async-start(), calls=%async_computation.3 | async-start | bytes 262144 | tf_op jit(solution)/shard_map/psum | solution.py:88
  187.4 19.5 %collective-permute-start.5 = (bf16[512,128]{1,0:T(8,128)(2,1)S(1)}, bf16[512,128]{1,0:T(8,128)(2,1)S(1)}, u32[]{:S(2)}, u32[]{:S(2)}) collective-permute-start(bf16[512,128]{1,0:T(8,128)(2,1)S(1)} %bitcast.69), channel_id=1, source_target_pairs={{0,3},{1,4},{2,5},{3,6},{4,7},{5,8},{6,9},{7,10},{8,11},{9,12},{10... | collective-permute-start | bytes 393224 | tf_op jit(solution)/shard_map/ppermute | solution.py:11
  187.5 28.0 %copy-start.1 = (bf16[512,128]{1,0:T(8,128)(2,1)S(1)}, bf16[512,128]{1,0:T(8,128)(2,1)}, u32[]{:S(2)}) copy-start(bf16[512,128]{1,0:T(8,128)(2,1)} %param.13) | copy-start | bytes 393220
  187.5 28.2 %copy-start.2 = (bf16[512,256]{1,0:T(8,128)(2,1)S(1)}, bf16[512,256]{1,0:T(8,128)(2,1)}, u32[]{:S(2)}) copy-start(bf16[512,256]{1,0:T(8,128)(2,1)} %param.21) | copy-start | bytes 786436
  187.5 28.2 %copy-start.3 = (f32[256]{0:T(256)S(1)}, f32[256]{0:T(256)}, u32[]{:S(2)}) copy-start(f32[256]{0:T(256)} %param.20) | copy-start | bytes 3076
  201.9 7.3 %collective-permute-start = (bf16[512,128]{1,0:T(8,128)(2,1)S(1)}, bf16[512,128]{1,0:T(8,128)(2,1)S(1)}, u32[]{:S(2)}, u32[]{:S(2)}) collective-permute-start(bf16[512,128]{1,0:T(8,128)(2,1)S(1)} %bitcast.68), channel_id=1, source_target_pairs={{0,29},{1,30},{2,31},{3,0},{4,1},{5,2},{6,3},{7,4},{8,5},{9,6},{10... | collective-permute-start | bytes 393224 | tf_op jit(solution)/shard_map/ppermute | solution.py:11
  203.6 9.7 %collective-permute-start.4 = (bf16[512,128]{1,0:T(8,128)(2,1)S(1)}, bf16[512,128]{1,0:T(8,128)(2,1)S(1)}, u32[]{:S(2)}, u32[]{:S(2)}) collective-permute-start(bf16[512,128]{1,0:T(8,128)(2,1)S(1)} %bitcast.67), channel_id=1, source_target_pairs={{0,2},{1,3},{2,4},{3,5},{4,6},{5,7},{6,8},{7,9},{8,10},{9,11},{10,... | collective-permute-start | bytes 393224 | tf_op jit(solution)/shard_map/ppermute | solution.py:11
  204.2 9.1 %collective-permute-start.3 = (bf16[512,128]{1,0:T(8,128)(2,1)S(1)}, bf16[512,128]{1,0:T(8,128)(2,1)S(1)}, u32[]{:S(2)}, u32[]{:S(2)}) collective-permute-start(bf16[512,128]{1,0:T(8,128)(2,1)S(1)} %bitcast.66), channel_id=1, source_target_pairs={{0,1},{1,2},{2,3},{3,4},{4,5},{5,6},{6,7},{7,8},{8,9},{9,10},{10,1... | collective-permute-start | bytes 393224 | tf_op jit(solution)/shard_map/ppermute | solution.py:11
  204.2 9.1 %collective-permute-start.2 = (bf16[512,128]{1,0:T(8,128)(2,1)S(1)}, bf16[512,128]{1,0:T(8,128)(2,1)S(1)}, u32[]{:S(2)}, u32[]{:S(2)}) collective-permute-start(bf16[512,128]{1,0:T(8,128)(2,1)S(1)} %bitcast.65), channel_id=1, source_target_pairs={{0,31},{1,0},{2,1},{3,2},{4,3},{5,4},{6,5},{7,6},{8,7},{9,8},{10,9... | collective-permute-start | bytes 393224 | tf_op jit(solution)/shard_map/ppermute | solution.py:11
  206.9 8.6 %collective-permute-start.1 = (bf16[512,128]{1,0:T(8,128)(2,1)S(1)}, bf16[512,128]{1,0:T(8,128)(2,1)S(1)}, u32[]{:S(2)}, u32[]{:S(2)}) collective-permute-start(bf16[512,128]{1,0:T(8,128)(2,1)S(1)} %bitcast.64), channel_id=1, source_target_pairs={{0,30},{1,31},{2,0},{3,1},{4,2},{5,3},{6,4},{7,5},{8,6},{9,7},{10,... | collective-permute-start | bytes 393224 | tf_op jit(solution)/shard_map/ppermute | solution.py:11
  217.0 19.1 %collective-permute-start.11 = (bf16[512,128]{1,0:T(8,128)(2,1)S(1)}, bf16[512,128]{1,0:T(8,128)(2,1)S(1)}, u32[]{:S(2)}, u32[]{:S(2)}) collective-permute-start(bf16[512,128]{1,0:T(8,128)(2,1)S(1)} %fusion.6), channel_id=1, source_target_pairs={{0,29},{1,30},{2,31},{3,0},{4,1},{5,2},{6,3},{7,4},{8,5},{9,6},{10... | collective-permute-start | bytes 393224 | tf_op jit(solution)/shard_map/ppermute | solution.py:11
  217.9 18.2 %collective-permute-start.10 = (bf16[512,128]{1,0:T(8,128)(2,1)S(1)}, bf16[512,128]{1,0:T(8,128)(2,1)S(1)}, u32[]{:S(2)}, u32[]{:S(2)}) collective-permute-start(bf16[512,128]{1,0:T(8,128)(2,1)S(1)} %fusion.6), channel_id=1, source_target_pairs={{0,30},{1,31},{2,0},{3,1},{4,2},{5,3},{6,4},{7,5},{8,6},{9,7},{10,... | collective-permute-start | bytes 393224 | tf_op jit(solution)/shard_map/ppermute | solution.py:11
  219.0 17.1 %collective-permute-start.9 = (bf16[512,128]{1,0:T(8,128)(2,1)S(1)}, bf16[512,128]{1,0:T(8,128)(2,1)S(1)}, u32[]{:S(2)}, u32[]{:S(2)}) collective-permute-start(bf16[512,128]{1,0:T(8,128)(2,1)S(1)} %fusion.6), channel_id=1, source_target_pairs={{0,31},{1,0},{2,1},{3,2},{4,3},{5,4},{6,5},{7,6},{8,7},{9,8},{10,9... | collective-permute-start | bytes 393224 | tf_op jit(solution)/shard_map/ppermute | solution.py:11
  222.3 13.7 %collective-permute-start.8 = (bf16[512,128]{1,0:T(8,128)(2,1)S(1)}, bf16[512,128]{1,0:T(8,128)(2,1)S(1)}, u32[]{:S(2)}, u32[]{:S(2)}) collective-permute-start(bf16[512,128]{1,0:T(8,128)(2,1)S(1)} %fusion.6), channel_id=1, source_target_pairs={{0,1},{1,2},{2,3},{3,4},{4,5},{5,6},{6,7},{7,8},{8,9},{9,10},{10,1... | collective-permute-start | bytes 393224 | tf_op jit(solution)/shard_map/ppermute | solution.py:11
  222.3 6.7 %collective-permute-start.6 = (bf16[512,128]{1,0:T(8,128)(2,1)S(1)}, bf16[512,128]{1,0:T(8,128)(2,1)S(1)}, u32[]{:S(2)}, u32[]{:S(2)}) collective-permute-start(bf16[512,128]{1,0:T(8,128)(2,1)S(1)} %fusion.6), channel_id=1, source_target_pairs={{0,3},{1,4},{2,5},{3,6},{4,7},{5,8},{6,9},{7,10},{8,11},{9,12},{10... | collective-permute-start | bytes 393224 | tf_op jit(solution)/shard_map/ppermute | solution.py:11
  223.9 325.1 %reduce-scatter.2.cloned.1.call-start = ((), (), s32[]{:S(2)}) async-start(), calls=%async_computation.2 | async-start | bytes 1179648 | tf_op jit(solution)/shard_map/reduce_scatter | solution.py:99
  229.0 7.0 %collective-permute-start.7 = (bf16[512,128]{1,0:T(8,128)(2,1)S(1)}, bf16[512,128]{1,0:T(8,128)(2,1)S(1)}, u32[]{:S(2)}, u32[]{:S(2)}) collective-permute-start(bf16[512,128]{1,0:T(8,128)(2,1)S(1)} %fusion.6), channel_id=1, source_target_pairs={{0,2},{1,3},{2,4},{3,5},{4,6},{5,7},{6,8},{7,9},{8,10},{9,11},{10,... | collective-permute-start | bytes 393224 | tf_op jit(solution)/shard_map/ppermute | solution.py:11
Sparse Core Ops, SparseCore 0:
  11.2 53.9 all-gather.1
  224.0 245.4 all-reduce.1
  473.4 75.5 reduce-scatter.1
where the time goes:
time: 561 us; the launch traced here: 557 us
  waiting for transfers between devices  189 us (34%)
  other arithmetic  164 us (29%)
  blocking collectives  75.9 us (14%)
  matrix products  55.7 us (10%)
  local copies, waits for them, and re-layouts  42.9 us (8%)
  between operations  14.6 us (3%)
  starting transfers between devices  14.4 us (3%)
    scatter-add x16, other arithmetic, add_block(): jax.ops.segment_sum(products, segment_part, segment_total + 1)  105 us
    reduce_scatter x1, waiting for transfers between devices, on_device(): lax.psum_scatter(column_part.reshape(rep_count * row_count, feat_width).a...  77.9 us
    psum x1, blocking collectives, on_device(): weight_sum, bias_sum = lax.psum((local_weight, local_bias), ('rep', 'blk'))  75.9 us
    dot_general x16, matrix products, add_block(): jnp.einsum(pattern, weights_part, source_tiles[gather_part], preferred_el...  53.5 us
    all_gather x1, waiting for transfers between devices, on_device(): source_rows = lax.all_gather(scaled, 'rep', axis=0, tiled=True)  53.4 us
    add x16, other arithmetic, add_block(): running + jax.ops.segment_sum(products, segment_part, segment_total + 1)[...  46.3 us
    psum x1, waiting for transfers between devices, on_device(): weight_sum, bias_sum = lax.psum((local_weight, local_bias), ('rep', 'blk'))  41.1 us
    gather x16, local copies, waits for them, and re-layouts, add_block(): source_tiles[gather_part]  22.5 us
  transfers between devices with their start and end apart: 15, of which 7 were waited for; matrix products, arithmetic and copies ran while one was open for 24% of the time, Pallas kernels for 0%

commit v1 on v0

--- a/solution.py
+++ b/solution.py
@@ -4,6 +4,14 @@
 from jax.sharding import PartitionSpec as P
 
 REACH = 3
+
+
+def _match_sources_all(v0):
+    mat_out = jnp.concatenate(
+        lax.all_to_all(jnp.stack([v0 for _ in range(lax.psum(1, "rep"))], axis=0), "rep", 0, 0),
+        axis=0,
+    )
+    return mat_out
 
 
 def shifted(value, axis, by):
@@ -63,7 +71,7 @@
 
     node_norm = node_scale(degrees)
     scaled = (node_norm[:, None] * features.astype(jnp.float32)).astype(jnp.bfloat16)
-    source_rows = lax.all_gather(scaled, "rep", axis=0, tiled=True)
+    source_rows = _match_sources_all(scaled)
     source_tiles = source_rows.reshape(column_tiles, tile_size, feat_width)
     partial_value = tile_pass(source_tiles, cols_dev, window_seg, window_tiles, "tab,tbf->taf")
     partial_value = partial_value.reshape(window_blocks, row_count, feat_width)

time: 561 us -> 445 us (0.79)
  waiting for transfers between devices: 189 us -> 69.9 us
  starting transfers between devices: 14.4 us -> 24.7 us
  local copies, waits for them, and re-layouts: 42.9 us -> 34.2 us
    reduce_scatter x1, waiting for transfers between devices: 77.9 us -> 0.01 us  [on_device(): lax.psum_scatter(column_part.reshape(rep_count * row_count, feat_width).a...]
    all_gather x1 -> x0, waiting for transfers between devices: 53.4 us -> none  [on_device(): source_rows = lax.all_gather(scaled, 'rep', axis=0, tiled=True)]
    all_to_all x0 -> x1, waiting for transfers between devices: none -> 16.4 us  [_match_sources_all(): lax.all_to_all(jnp.stack([v0 for _ in range(lax.psum(1, 'rep'))], axis=0)...]
    gather x16, local copies, waits for them, and re-layouts: 22.5 us -> 12.8 us  [add_block(): source_tiles[gather_part]]
    all_to_all x0 -> x1, starting transfers between devices: none -> 6.93 us  [_match_sources_all(): lax.all_to_all(jnp.stack([v0 for _ in range(lax.psum(1, 'rep'))], axis=0)...]
    unnamed x15 -> x19, local copies, waits for them, and re-layouts: 14.6 us -> 14.6 us
  transfers between devices with their start and end apart: 15 -> 15, of which waited for: 7 -> 6; matrix products, arithmetic and copies ran while one was open for 24% -> 31% of each run, Pallas kernels for 0% -> 0%
where the time goes in v1:
time: 445 us; the launch traced here: 440 us
  other arithmetic  162 us (36%)
  blocking collectives  75.7 us (17%)
  waiting for transfers between devices  69.9 us (16%)
  matrix products  55.7 us (13%)
  local copies, waits for them, and re-layouts  34.2 us (8%)
  starting transfers between devices  24.7 us (6%)
  between operations  16.4 us (4%)
    scatter-add x16, other arithmetic, add_block(): jax.ops.segment_sum(products, segment_part, segment_total + 1)  105 us
    psum x1, blocking collectives, on_device(): weight_sum, bias_sum = lax.psum((local_weight, local_bias), ('rep', 'blk'))  75.7 us
    dot_general x16, matrix products, add_block(): jnp.einsum(pattern, weights_part, source_tiles[gather_part], preferred_el...  53.5 us
    add x16, other arithmetic, add_block(): running + jax.ops.segment_sum(products, segment_part, segment_total + 1)[...  46.3 us
    psum x1, waiting for transfers between devices, on_device(): weight_sum, bias_sum = lax.psum((local_weight, local_bias), ('rep', 'blk'))  38.9 us
    ppermute x12, starting transfers between devices, shifted(): lax.ppermute(value, axis, [(i, (i + by) % length) for i in range(length)])  17.7 us
    all_to_all x1, waiting for transfers between devices, _match_sources_all(): lax.all_to_all(jnp.stack([v0 for _ in range(lax.psum(1, 'rep'))], axis=0)...  16.4 us
    ppermute x12, waiting for transfers between devices, shifted(): lax.ppermute(value, axis, [(i, (i + by) % length) for i in range(length)])  14.6 us
  transfers between devices with their start and end apart: 15, of which 6 were waited for; matrix products, arithmetic and copies ran while one was open for 31% of the time, Pallas kernels for 0%

profile of v1, /device:TPU:32, one launch (start us, length us, event | category | flops | bytes accessed | tf_op | source)
XLA Modules:
  0.0 439.5 jit_solution(10149008281035345085)
XLA Ops:
  10.9 6.9 %all-to-all-start = ((bf16[8,512,128]{2,1,0:T(8,128)(2,1)}), bf16[8,512,128]{2,1,0:T(8,128)(2,1)S(1)}, u32[]{:S(2)}, u32[]{:S(2)}) async-start(bf16[8,512,128]{2,1,0:T(8,128)(2,1)} %stack.35), calls=%async_computation | async-start | bytes 2097152 | tf_op jit(solution)/shard_map/all_to_all | solution.py:11
  18.6 16.4 %all-to-all-done = bf16[8,512,128]{2,1,0:T(8,128)(2,1)S(1)} async-done(((bf16[8,512,128]{2,1,0:T(8,128)(2,1)}), bf16[8,512,128]{2,1,0:T(8,128)(2,1)S(1)}, u32[]{:S(2)}, u32[]{:S(2)}) %all-to-all-start) | async-done | bytes 1048608 | tf_op jit(solution)/shard_map/all_to_all | solution.py:11
  35.0 110.7 %while.28 = (s32[]{:T(128)}, f32[28,128,128]{2,1,0:T(8,128)}, s32[320]{0:T(512)S(1)}, bf16[320,128,128]{2,1,0:T(8,128)(2,1)}, s32[320]{0:T(512)S(1)}, /*index=5*...) while((s32[]{:T(128)}, f32[28,128,128]{2,1,0:T(8,128)}, ...), condition=%wide.region_2.3_spmd.clone, body=%wide.region_0.2_spmd.clone.sunk | while | flops 169346176 | bytes 23139612 | solution.py:70
  39.5 6.5 %scatter_fusion = f32[29,128,128]{2,1,0:T(8,128)S(1)} fusion(f32[29,128,128]{2,1,0:T(8,128)S(1)} %broadcast.129, s32[40]{0:T(128)S(1)} %dynamic_slice.62, f32[40,128,128]{2,1,0:T(8,128)} %fusion.44), kind=kCustom, calls=%fused_computation.2.clone.clone.1 | custom fusion | flops 655360 | bytes 7864480 | tf_op jit(solution)/shard_map/while/body/eval_jaxpr/scatter-add | solution.py:66
  52.1 6.5 %scatter_fusion = f32[29,128,128]{2,1,0:T(8,128)S(1)} fusion(f32[29,128,128]{2,1,0:T(8,128)S(1)} %broadcast.129, s32[40]{0:T(128)S(1)} %dynamic_slice.62, f32[40,128,128]{2,1,0:T(8,128)} %fusion.44), kind=kCustom, calls=%fused_computation.2.clone.clone.1 | custom fusion | flops 655360 | bytes 7864480 | tf_op jit(solution)/shard_map/while/body/eval_jaxpr/scatter-add | solution.py:66
  66.1 6.5 %scatter_fusion = f32[29,128,128]{2,1,0:T(8,128)S(1)} fusion(f32[29,128,128]{2,1,0:T(8,128)S(1)} %broadcast.129, s32[40]{0:T(128)S(1)} %dynamic_slice.62, f32[40,128,128]{2,1,0:T(8,128)} %fusion.44), kind=kCustom, calls=%fused_computation.2.clone.clone.1 | custom fusion | flops 655360 | bytes 7864480 | tf_op jit(solution)/shard_map/while/body/eval_jaxpr/scatter-add | solution.py:66
  80.1 6.5 %scatter_fusion = f32[29,128,128]{2,1,0:T(8,128)S(1)} fusion(f32[29,128,128]{2,1,0:T(8,128)S(1)} %broadcast.129, s32[40]{0:T(128)S(1)} %dynamic_slice.62, f32[40,128,128]{2,1,0:T(8,128)} %fusion.44), kind=kCustom, calls=%fused_computation.2.clone.clone.1 | custom fusion | flops 655360 | bytes 7864480 | tf_op jit(solution)/shard_map/while/body/eval_jaxpr/scatter-add | solution.py:66
  94.1 6.5 %scatter_fusion = f32[29,128,128]{2,1,0:T(8,128)S(1)} fusion(f32[29,128,128]{2,1,0:T(8,128)S(1)} %broadcast.129, s32[40]{0:T(128)S(1)} %dynamic_slice.62, f32[40,128,128]{2,1,0:T(8,128)} %fusion.44), kind=kCustom, calls=%fused_computation.2.clone.clone.1 | custom fusion | flops 655360 | bytes 7864480 | tf_op jit(solution)/shard_map/while/body/eval_jaxpr/scatter-add | solution.py:66
  108.2 6.5 %scatter_fusion = f32[29,128,128]{2,1,0:T(8,128)S(1)} fusion(f32[29,128,128]{2,1,0:T(8,128)S(1)} %broadcast.129, s32[40]{0:T(128)S(1)} %dynamic_slice.62, f32[40,128,128]{2,1,0:T(8,128)} %fusion.44), kind=kCustom, calls=%fused_computation.2.clone.clone.1 | custom fusion | flops 655360 | bytes 7864480 | tf_op jit(solution)/shard_map/while/body/eval_jaxpr/scatter-add | solution.py:66
  122.2 6.5 %scatter_fusion = f32[29,128,128]{2,1,0:T(8,128)S(1)} fusion(f32[29,128,128]{2,1,0:T(8,128)S(1)} %broadcast.129, s32[40]{0:T(128)S(1)} %dynamic_slice.62, f32[40,128,128]{2,1,0:T(8,128)} %fusion.44), kind=kCustom, calls=%fused_computation.2.clone.clone.1 | custom fusion | flops 655360 | bytes 7864480 | tf_op jit(solution)/shard_map/while/body/eval_jaxpr/scatter-add | solution.py:66
  136.2 6.5 %scatter_fusion = f32[29,128,128]{2,1,0:T(8,128)S(1)} fusion(f32[29,128,128]{2,1,0:T(8,128)S(1)} %broadcast.129, s32[40]{0:T(128)S(1)} %dynamic_slice.62, f32[40,128,128]{2,1,0:T(8,128)} %fusion.44), kind=kCustom, calls=%fused_computation.2.clone.clone.1 | custom fusion | flops 655360 | bytes 7864480 | tf_op jit(solution)/shard_map/while/body/eval_jaxpr/scatter-add | solution.py:66
  147.6 14.4 %copy.13 = bf16[1,1,320,128,128]{3,4,2,1,0:T(8,128)(2,1)} copy(bf16[1,1,320,128,128]{4,3,2,1,0:T(8,128)(2,1)} %bitcast.61) | data formatting | bytes 20971520 | tf_op args[2]
  170.2 3.5 collective-permute-done.4
  181.1 3.4 collective-permute-start.9
  185.5 4.3 collective-permute-done.6
  189.8 3.4 collective-permute-start.7
  193.2 4.5 %collective-permute-done.7 = bf16[512,128]{1,0:T(8,128)(2,1)S(1)} collective-permute-done((bf16[512,128]{1,0:T(8,128)(2,1)S(1)}, bf16[512,128]{1,0:T(8,128)(2,1)S(1)}, u32[]{:S(2)}, u32[]{:S(2)}) %collective-permute-start.7) | collective-permute-done | bytes 131104 | tf_op jit(solution)/shard_map/ppermute | solution.py:19
  197.9 113.0 %while.29 = (s32[]{:T(128)}, f32[32,128,128]{2,1,0:T(8,128)}, s32[320]{0:T(512)S(1)}, bf16[320,128,128]{1,2,0:T(8,128)(2,1)}, s32[320]{0:T(512)S(1)}, /*index=5*...) while((s32[]{:T(128)}, f32[32,128,128]{2,1,0:T(8,128)}, ...), condition=%wide.region_5.6_spmd.clone, body=%wide.region_3.5_spmd.clone.sunk | while | flops 169477248 | bytes 24188188 | solution.py:70
  198.8 3.4 fusion.47
  202.4 6.6 %scatter_fusion.1 = f32[33,128,128]{2,1,0:T(8,128)S(1)} fusion(f32[33,128,128]{2,1,0:T(8,128)S(1)} %broadcast.136, s32[40]{0:T(128)S(1)} %dynamic_slice.65, f32[40,128,128]{2,1,0:T(8,128)} %fusion.47), kind=kCustom, calls=%fused_computation.3.clone.clone.1 | custom fusion | flops 655360 | bytes 7864480 | tf_op jit(solution)/shard_map/while/body/eval_jaxpr/scatter-add | solution.py:66
  211.6 3.4 fusion.47
  215.2 6.6 %scatter_fusion.1 = f32[33,128,128]{2,1,0:T(8,128)S(1)} fusion(f32[33,128,128]{2,1,0:T(8,128)S(1)} %broadcast.136, s32[40]{0:T(128)S(1)} %dynamic_slice.65, f32[40,128,128]{2,1,0:T(8,128)} %fusion.47), kind=kCustom, calls=%fused_computation.3.clone.clone.1 | custom fusion | flops 655360 | bytes 7864480 | tf_op jit(solution)/shard_map/while/body/eval_jaxpr/scatter-add | solution.py:66
  225.9 3.4 fusion.47
  229.5 6.6 %scatter_fusion.1 = f32[33,128,128]{2,1,0:T(8,128)S(1)} fusion(f32[33,128,128]{2,1,0:T(8,128)S(1)} %broadcast.136, s32[40]{0:T(128)S(1)} %dynamic_slice.65, f32[40,128,128]{2,1,0:T(8,128)} %fusion.47), kind=kCustom, calls=%fused_computation.3.clone.clone.1 | custom fusion | flops 655360 | bytes 7864480 | tf_op jit(solution)/shard_map/while/body/eval_jaxpr/scatter-add | solution.py:66
  243.9 6.6 %scatter_fusion.1 = f32[33,128,128]{2,1,0:T(8,128)S(1)} fusion(f32[33,128,128]{2,1,0:T(8,128)S(1)} %broadcast.136, s32[40]{0:T(128)S(1)} %dynamic_slice.65, f32[40,128,128]{2,1,0:T(8,128)} %fusion.47), kind=kCustom, calls=%fused_computation.3.clone.clone.1 | custom fusion | flops 655360 | bytes 7864480 | tf_op jit(solution)/shard_map/while/body/eval_jaxpr/scatter-add | solution.py:66
  258.2 6.6 %scatter_fusion.1 = f32[33,128,128]{2,1,0:T(8,128)S(1)} fusion(f32[33,128,128]{2,1,0:T(8,128)S(1)} %broadcast.136, s32[40]{0:T(128)S(1)} %dynamic_slice.65, f32[40,128,128]{2,1,0:T(8,128)} %fusion.47), kind=kCustom, calls=%fused_computation.3.clone.clone.1 | custom fusion | flops 655360 | bytes 7864480 | tf_op jit(solution)/shard_map/while/body/eval_jaxpr/scatter-add | solution.py:66
  272.5 6.6 %scatter_fusion.1 = f32[33,128,128]{2,1,0:T(8,128)S(1)} fusion(f32[33,128,128]{2,1,0:T(8,128)S(1)} %broadcast.136, s32[40]{0:T(128)S(1)} %dynamic_slice.65, f32[40,128,128]{2,1,0:T(8,128)} %fusion.47), kind=kCustom, calls=%fused_computation.3.clone.clone.1 | custom fusion | flops 655360 | bytes 7864480 | tf_op jit(solution)/shard_map/while/body/eval_jaxpr/scatter-add | solution.py:66
  286.8 6.5 %scatter_fusion.1 = f32[33,128,128]{2,1,0:T(8,128)S(1)} fusion(f32[33,128,128]{2,1,0:T(8,128)S(1)} %broadcast.136, s32[40]{0:T(128)S(1)} %dynamic_slice.65, f32[40,128,128]{2,1,0:T(8,128)} %fusion.47), kind=kCustom, calls=%fused_computation.3.clone.clone.1 | custom fusion | flops 655360 | bytes 7864480 | tf_op jit(solution)/shard_map/while/body/eval_jaxpr/scatter-add | solution.py:66
  297.5 3.4 fusion.47
  301.1 6.5 %scatter_fusion.1 = f32[33,128,128]{2,1,0:T(8,128)S(1)} fusion(f32[33,128,128]{2,1,0:T(8,128)S(1)} %broadcast.136, s32[40]{0:T(128)S(1)} %dynamic_slice.65, f32[40,128,128]{2,1,0:T(8,128)} %fusion.47), kind=kCustom, calls=%fused_computation.3.clone.clone.1 | custom fusion | flops 655360 | bytes 7864480 | tf_op jit(solution)/shard_map/while/body/eval_jaxpr/scatter-add | solution.py:66
  313.6 75.7 %psum.15 = f32[256]{0:T(256)S(1)} all-reduce(f32[256]{0:T(256)S(1)} %get-tuple-element.296), channel_id=1, replica_groups=mesh['rep'=8,'blk'=32] {'rep','blk'}, use_global_device_ids=true, to_apply=%region_9.10 | all-reduce | flops 256 | bytes 2048 | tf_op jit(solution)/shard_map/psum | solution.py:96
  389.9 38.9 %all-reduce.2.cloned.1.call-done = f32[128,256]{1,0:T(8,128)} async-done(((f32[128,256]{1,0:T(8,128)}), f32[128,256]{1,0:T(8,128)}) %all-reduce.2.cloned.1.call-update) | async-done | bytes 131088 | tf_op jit(solution)/shard_map/psum | solution.py:96
  (171 shorter events, 133.2 us)
Async XLA Ops:
  8.0 168.1 %copy-start = (bf16[128,256]{1,0:T(8,128)(2,1)S(1)}, bf16[128,256]{1,0:T(8,128)(2,1)}, u32[]{:S(2)}) copy-start(bf16[128,256]{1,0:T(8,128)(2,1)} %param.19) | copy-start | bytes 196612
  8.0 10.5 %copy-start.2 = (s32[1,1,320]{2,1,0:T(1,128)S(1)}, s32[1,1,320]{2,1,0:T(1,128)}, u32[]{:S(2)}) copy-start(s32[1,1,320]{2,1,0:T(1,128)} %param.17) | copy-start | bytes 3844
  8.0 10.5 %copy-start.3 = (s32[1,1,320]{2,1,0:T(1,128)S(1)}, s32[1,1,320]{2,1,0:T(1,128)}, u32[]{:S(2)}) copy-start(s32[1,1,320]{2,1,0:T(1,128)} %param.16) | copy-start | bytes 3844
  10.9 24.1 %all-to-all-start = ((bf16[8,512,128]{2,1,0:T(8,128)(2,1)}), bf16[8,512,128]{2,1,0:T(8,128)(2,1)S(1)}, u32[]{:S(2)}, u32[]{:S(2)}) async-start(bf16[8,512,128]{2,1,0:T(8,128)(2,1)} %stack.35), calls=%async_computation | async-start | bytes 2097152 | tf_op jit(solution)/shard_map/all_to_all | solution.py:11
  17.8 411.0 %all-reduce.2.cloned.1.call-start = ((), (), s32[]{:S(2)}) async-start(), calls=%async_computation.3 | async-start | bytes 262144 | tf_op jit(solution)/shard_map/psum | solution.py:96
  147.4 19.5 %collective-permute-start.5 = (bf16[512,128]{1,0:T(8,128)(2,1)S(1)}, bf16[512,128]{1,0:T(8,128)(2,1)S(1)}, u32[]{:S(2)}, u32[]{:S(2)}) collective-permute-start(bf16[512,128]{1,0:T(8,128)(2,1)S(1)} %bitcast.69), channel_id=1, source_target_pairs={{0,3},{1,4},{2,5},{3,6},{4,7},{5,8},{6,9},{7,10},{8,11},{9,12},{10... | collective-permute-start | bytes 393224 | tf_op jit(solution)/shard_map/ppermute | solution.py:19
  147.5 28.4 %copy-start.1 = (bf16[512,128]{1,0:T(8,128)(2,1)S(1)}, bf16[512,128]{1,0:T(8,128)(2,1)}, u32[]{:S(2)}) copy-start(bf16[512,128]{1,0:T(8,128)(2,1)} %param.13) | copy-start | bytes 393220
  147.5 28.5 %copy-start.4 = (bf16[512,256]{1,0:T(8,128)(2,1)S(1)}, bf16[512,256]{1,0:T(8,128)(2,1)}, u32[]{:S(2)}) copy-start(bf16[512,256]{1,0:T(8,128)(2,1)} %param.21) | copy-start | bytes 786436
  147.6 28.5 %copy-start.5 = (f32[256]{0:T(256)S(1)}, f32[256]{0:T(256)}, u32[]{:S(2)}) copy-start(f32[256]{0:T(256)} %param.20) | copy-start | bytes 3076
  162.0 8.2 %collective-permute-start = (bf16[512,128]{1,0:T(8,128)(2,1)S(1)}, bf16[512,128]{1,0:T(8,128)(2,1)S(1)}, u32[]{:S(2)}, u32[]{:S(2)}) collective-permute-start(bf16[512,128]{1,0:T(8,128)(2,1)S(1)} %bitcast.68), channel_id=1, source_target_pairs={{0,29},{1,30},{2,31},{3,0},{4,1},{5,2},{6,3},{7,4},{8,5},{9,6},{10... | collective-permute-start | bytes 393224 | tf_op jit(solution)/shard_map/ppermute | solution.py:19
  163.7 10.0 %collective-permute-start.4 = (bf16[512,128]{1,0:T(8,128)(2,1)S(1)}, bf16[512,128]{1,0:T(8,128)(2,1)S(1)}, u32[]{:S(2)}, u32[]{:S(2)}) collective-permute-start(bf16[512,128]{1,0:T(8,128)(2,1)S(1)} %bitcast.67), channel_id=1, source_target_pairs={{0,2},{1,3},{2,4},{3,5},{4,6},{5,7},{6,8},{7,9},{8,10},{9,11},{10,... | collective-permute-start | bytes 393224 | tf_op jit(solution)/shard_map/ppermute | solution.py:19
  164.3 9.4 %collective-permute-start.3 = (bf16[512,128]{1,0:T(8,128)(2,1)S(1)}, bf16[512,128]{1,0:T(8,128)(2,1)S(1)}, u32[]{:S(2)}, u32[]{:S(2)}) collective-permute-start(bf16[512,128]{1,0:T(8,128)(2,1)S(1)} %bitcast.66), channel_id=1, source_target_pairs={{0,1},{1,2},{2,3},{3,4},{4,5},{5,6},{6,7},{7,8},{8,9},{9,10},{10,1... | collective-permute-start | bytes 393224 | tf_op jit(solution)/shard_map/ppermute | solution.py:19
  164.3 9.4 %collective-permute-start.2 = (bf16[512,128]{1,0:T(8,128)(2,1)S(1)}, bf16[512,128]{1,0:T(8,128)(2,1)S(1)}, u32[]{:S(2)}, u32[]{:S(2)}) collective-permute-start(bf16[512,128]{1,0:T(8,128)(2,1)S(1)} %bitcast.65), channel_id=1, source_target_pairs={{0,31},{1,0},{2,1},{3,2},{4,3},{5,4},{6,5},{7,6},{8,7},{9,8},{10,9... | collective-permute-start | bytes 393224 | tf_op jit(solution)/shard_map/ppermute | solution.py:19
  166.9 9.0 %collective-permute-start.1 = (bf16[512,128]{1,0:T(8,128)(2,1)S(1)}, bf16[512,128]{1,0:T(8,128)(2,1)S(1)}, u32[]{:S(2)}, u32[]{:S(2)}) collective-permute-start(bf16[512,128]{1,0:T(8,128)(2,1)S(1)} %bitcast.64), channel_id=1, source_target_pairs={{0,30},{1,31},{2,0},{3,1},{4,2},{5,3},{6,4},{7,5},{8,6},{9,7},{10,... | collective-permute-start | bytes 393224 | tf_op jit(solution)/shard_map/ppermute | solution.py:19
  177.4 20.4 %collective-permute-start.11 = (bf16[512,128]{1,0:T(8,128)(2,1)S(1)}, bf16[512,128]{1,0:T(8,128)(2,1)S(1)}, u32[]{:S(2)}, u32[]{:S(2)}) collective-permute-start(bf16[512,128]{1,0:T(8,128)(2,1)S(1)} %fusion.6), channel_id=1, source_target_pairs={{0,29},{1,30},{2,31},{3,0},{4,1},{5,2},{6,3},{7,4},{8,5},{9,6},{10... | collective-permute-start | bytes 393224 | tf_op jit(solution)/shard_map/ppermute | solution.py:19
  179.3 18.5 %collective-permute-start.10 = (bf16[512,128]{1,0:T(8,128)(2,1)S(1)}, bf16[512,128]{1,0:T(8,128)(2,1)S(1)}, u32[]{:S(2)}, u32[]{:S(2)}) collective-permute-start(bf16[512,128]{1,0:T(8,128)(2,1)S(1)} %fusion.6), channel_id=1, source_target_pairs={{0,30},{1,31},{2,0},{3,1},{4,2},{5,3},{6,4},{7,5},{8,6},{9,7},{10,... | collective-permute-start | bytes 393224 | tf_op jit(solution)/shard_map/ppermute | solution.py:19
  181.1 16.6 %collective-permute-start.9 = (bf16[512,128]{1,0:T(8,128)(2,1)S(1)}, bf16[512,128]{1,0:T(8,128)(2,1)S(1)}, u32[]{:S(2)}, u32[]{:S(2)}) collective-permute-start(bf16[512,128]{1,0:T(8,128)(2,1)S(1)} %fusion.6), channel_id=1, source_target_pairs={{0,31},{1,0},{2,1},{3,2},{4,3},{5,4},{6,5},{7,6},{8,7},{9,8},{10,9... | collective-permute-start | bytes 393224 | tf_op jit(solution)/shard_map/ppermute | solution.py:19
  184.5 13.2 %collective-permute-start.8 = (bf16[512,128]{1,0:T(8,128)(2,1)S(1)}, bf16[512,128]{1,0:T(8,128)(2,1)S(1)}, u32[]{:S(2)}, u32[]{:S(2)}) collective-permute-start(bf16[512,128]{1,0:T(8,128)(2,1)S(1)} %fusion.6), channel_id=1, source_target_pairs={{0,1},{1,2},{2,3},{3,4},{4,5},{5,6},{6,7},{7,8},{8,9},{9,10},{10,1... | collective-permute-start | bytes 393224 | tf_op jit(solution)/shard_map/ppermute | solution.py:19
  184.5 5.3 %collective-permute-start.6 = (bf16[512,128]{1,0:T(8,128)(2,1)S(1)}, bf16[512,128]{1,0:T(8,128)(2,1)S(1)}, u32[]{:S(2)}, u32[]{:S(2)}) collective-permute-start(bf16[512,128]{1,0:T(8,128)(2,1)S(1)} %fusion.6), channel_id=1, source_target_pairs={{0,3},{1,4},{2,5},{3,6},{4,7},{5,8},{6,9},{7,10},{8,11},{9,12},{10... | collective-permute-start | bytes 393224 | tf_op jit(solution)/shard_map/ppermute | solution.py:19
  185.4 245.0 %reduce-scatter.2.cloned.1.call-start = ((), (), s32[]{:S(2)}) async-start(), calls=%async_computation.2 | async-start | bytes 1179648 | tf_op jit(solution)/shard_map/reduce_scatter | solution.py:107
  189.8 7.9 %collective-permute-start.7 = (bf16[512,128]{1,0:T(8,128)(2,1)S(1)}, bf16[512,128]{1,0:T(8,128)(2,1)S(1)}, u32[]{:S(2)}, u32[]{:S(2)}) collective-permute-start(bf16[512,128]{1,0:T(8,128)(2,1)S(1)} %fusion.6), channel_id=1, source_target_pairs={{0,2},{1,3},{2,4},{3,5},{4,6},{5,7},{6,8},{7,9},{8,10},{9,11},{10,... | collective-permute-start | bytes 393224 | tf_op jit(solution)/shard_map/ppermute | solution.py:19
Sparse Core Ops, SparseCore 0:
  185.5 243.2 all-reduce.1
Sparse Core Ops, SparseCore 1:
  313.7 76.2 reduce-scatter.1
